TPU v7x, 32 devices: a whole 2x2x4 slice. The times are simulated.
32 devices in a mesh: sub: 8 (over y, x, core), dir: 4 (over z).
Axes of the slice: x: 2, y: 2, z: 4, core: 2. Of those that a mesh axis runs over, the one named last changes fastest.
Arguments:
- fine_fields: float32 [8192, 2, 1024], P(('sub', 'dir')), may hold values from -6 to 6
- fine_octant: int32 [8192], P(('sub', 'dir')), may hold values from 0 to 7, as said below
- mid_octant: int32 [1024], P('sub'), may hold values from 0 to 7, as said below
- shift_fine: float32 [8, 4096], replicated, may hold values from -3.140625 to 3.140625
- shift_mid: float32 [8, 16384], replicated, may hold values from -3.140625 to 3.140625
- interp_theta_mid: float32 [64, 32], replicated, may hold values from -1 to 1
- interp_phi_mid: float32 [64, 32], replicated, may hold values from -1 to 1
- interp_theta_top: float32 [128, 64], replicated, may hold values from -0.75 to 0.75
- interp_phi_top: float32 [128, 64], replicated, may hold values from -0.75 to 0.75
- partners: int32 [128, 32], P('sub'), may hold values from 0 to 127, as said below
- translation: float32 [128, 32, 2, 16384], P('sub', None, None, 'dir'), may hold values from -0.0234375 to 0.0234375
Outputs:
- fine_incoming: float32 [8192, 2, 1024], P(('sub', 'dir'))
Inputs may be any that keep to these rules, and one draw needn't show every extreme that they name: `fine_octant`: each aligned group of 8 entries is a permutation of 0 to 7. `mid_octant`: each aligned group of 8 entries is a permutation of 0 to 7. `partners`: row t names 32 different top boxes, none of them t.
All inputs are finite; a program needn't handle non-finite values.
Results may differ from a plain program's by a relative error of at most 0.000096.
Values sent between devices are 32-bit elements; how exact they have to be, the bound alone decides.
A program may use at most 128 MiB of HBM per device.

v0:
```python
import functools

import jax
import jax.numpy as jnp
from jax import lax
from jax.experimental import pallas as pl
from jax.experimental.pallas import tpu as pltpu
from jax.sharding import PartitionSpec as P

LANES = 128
BF = jnp.bfloat16
F32 = jnp.float32


def split(x):
    hi = x.astype(BF)
    return hi, (x - hi.astype(F32)).astype(BF)


def mm(a, b):
    return jnp.dot(a, b, preferred_element_type=F32)


def wide_dot(x, w_hi, w_lo):
    hi, lo = split(x)
    return mm(hi, w_hi) + (mm(hi, w_lo) + mm(lo, w_hi))


def left3(a):
    hi, lo = split(a)
    return jnp.concatenate([hi, lo, hi], axis=1)


def right3(x):
    hi, lo = split(x)
    return jnp.concatenate([hi, hi, lo], axis=0)


def chunk_of(rows):
    return min(rows, 512)


def up_kernel(fine_oct, mid_oct, x_ref, wf_ref, af_ref, wt_ref, at_ref, cf_ref, sf_ref, ct_ref, st_ref,
              out_ref, y_ref, mid_ref, z_ref):
    pack = y_ref.shape[0]
    rows = y_ref.shape[1]
    theta_mid = cf_ref.shape[1]
    theta_fine = af_ref.shape[1]
    per = theta_fine // pack
    theta_top = ct_ref.shape[1]
    mids = mid_ref.shape[0] // theta_mid
    dirs, slots, _, band, _ = out_ref.shape
    half = LANES // 2

    wf_hi, wf_lo = split(wf_ref[...])
    step = chunk_of(rows)

    @pl.loop(0, rows // step)
    def _(i):
        base = pl.multiple_of(i * step, 8)
        re = x_ref[pl.ds(2 * base, step, stride=2), :]
        im = x_ref[pl.ds(2 * base + 1, step, stride=2), :]
        y = wide_dot(jnp.concatenate([re, im], axis=1), wf_hi, wf_lo)
        for a in range(pack):
            y_ref[a, pl.ds(base, step), :] = y[:, a * LANES:(a + 1) * LANES]

    a_mid = left3(af_ref[...])

    def box(b):
        start = pl.multiple_of(b * per, per)
        return jnp.concatenate([y_ref[a, pl.ds(start, per), :] for a in range(pack)], axis=0)

    def mid_step(m, carry):
        acc1 = jnp.zeros((theta_mid, LANES), F32)
        acc2 = jnp.zeros((theta_mid, LANES), F32)
        for i in range(0, 8, 2):
            b = m * 8 + i
            z = mm(a_mid, right3(jnp.concatenate([box(b), box(b + 1)], axis=1)))
            for side in range(2):
                o = fine_oct[b + side]
                part = z[:, side * LANES:(side + 1) * LANES]
                acc1 += part * cf_ref[o]
                acc2 += part * sf_ref[o]
        mid_ref[pl.ds(pl.multiple_of(m * theta_mid, theta_mid), theta_mid), :] = acc1 + pltpu.roll(acc2, half, 1)
        return carry

    lax.fori_loop(0, mids, mid_step, 0, unroll=2)

    wt_hi, wt_lo = split(wt_ref[...])
    mid_rows = mids * theta_mid
    step2 = chunk_of(mid_rows)

    @pl.loop(0, mid_rows // step2)
    def _(i):
        base = pl.multiple_of(i * step2, 8)
        z_ref[pl.ds(base, step2), :] = wide_dot(mid_ref[pl.ds(base, step2), :], wt_hi, wt_lo)

    a_top = left3(at_ref[...])
    out_ref[...] = jnp.zeros_like(out_ref)

    def top_step(m, carry):
        q = m // 8
        o = mid_oct[m]
        z = mm(a_top, right3(z_ref[pl.ds(pl.multiple_of(m * theta_mid, theta_mid), theta_mid), :]))
        for d in range(dirs):
            at = slice(d * band, (d + 1) * band)
            c, s = ct_ref[o, at, :], st_ref[o, at, :]
            re, im = z[at, :LANES], z[at, LANES:]
            out_ref[d, q, 0] += re * c - im * s
            out_ref[d, q, 1] += re * s + im * c
        return carry

    lax.fori_loop(0, mids, top_step, 0, unroll=2)


def down_kernel(fine_oct, mid_oct, r_ref, wf_ref, af_ref, wt_ref, at_ref, cf_ref, sf_ref, ct_ref, st_ref,
                out_ref, z_ref, mid_ref, y_ref):
    pack = y_ref.shape[0]
    rows = y_ref.shape[1]
    theta_mid = cf_ref.shape[1]
    theta_fine = af_ref.shape[0]
    per = theta_fine // pack
    mids = mid_ref.shape[0] // theta_mid
    dirs = r_ref.shape[0]
    half = LANES // 2

    a_hi, a_lo = split(at_ref[...])
    a_top = jnp.concatenate(
        [jnp.concatenate([a_hi, a_hi], axis=1), jnp.concatenate([a_lo, a_lo], axis=1)], axis=0)

    def top_step(m, carry):
        q = m // 8
        o = mid_oct[m]
        c, s = ct_ref[o], st_ref[o]
        re = jnp.concatenate([r_ref[d, q, 0] for d in range(dirs)], axis=0)
        im = jnp.concatenate([r_ref[d, q, 1] for d in range(dirs)], axis=0)
        hi, lo = split(jnp.concatenate([re * c + im * s, im * c - re * s], axis=1))
        z = mm(a_top, jnp.concatenate([hi, lo], axis=0))
        z_ref[pl.ds(pl.multiple_of(m * theta_mid, theta_mid), theta_mid), :] = z[:theta_mid] + z[theta_mid:]
        return carry

    lax.fori_loop(0, mids, top_step, 0, unroll=2)

    wt_hi, wt_lo = split(wt_ref[...])
    mid_rows = mids * theta_mid
    step2 = chunk_of(mid_rows)

    @pl.loop(0, mid_rows // step2)
    def _(i):
        base = pl.multiple_of(i * step2, 8)
        mid_ref[pl.ds(base, step2), :] = wide_dot(z_ref[pl.ds(base, step2), :], wt_hi, wt_lo)

    a_mid = left3(af_ref[...])

    def mid_step(m, carry):
        v = mid_ref[pl.ds(pl.multiple_of(m * theta_mid, theta_mid), theta_mid), :]
        turned = pltpu.roll(v, half, 1)
        for i in range(0, 8, 2):
            b = m * 8 + i
            both = []
            for side in range(2):
                o = fine_oct[b + side]
                both.append(v * cf_ref[o] + turned * sf_ref[o])
            z = mm(a_mid, right3(jnp.concatenate(both, axis=1)))
            for side in range(2):
                start = pl.multiple_of((b + side) * per, per)
                for a in range(pack):
                    y_ref[a, pl.ds(start, per), :] = z[a * per:(a + 1) * per, side * LANES:(side + 1) * LANES]
        return carry

    lax.fori_loop(0, mids, mid_step, 0, unroll=2)

    wf_hi, wf_lo = split(wf_ref[...])
    step = chunk_of(rows)

    @pl.loop(0, rows // step)
    def _(i):
        base = pl.multiple_of(i * step, 8)
        v = jnp.concatenate([y_ref[a, pl.ds(base, step), :] for a in range(pack)], axis=1)
        y = wide_dot(v, wf_hi, wf_lo)
        out_ref[pl.ds(2 * base, step, stride=2), :] = y[:, :LANES]
        out_ref[pl.ds(2 * base + 1, step, stride=2), :] = y[:, LANES:]


def translate_kernel(partners, p_ref, w_ref, out_ref):
    t = pl.program_id(0)
    band = p_ref.shape[2]

    def step(k, carry):
        re, im = carry
        n = partners[t, k]
        wr = w_ref[0, k, pl.ds(0, band, stride=2), :]
        wi = w_ref[0, k, pl.ds(1, band, stride=2), :]
        vr, vi = p_ref[n, 0], p_ref[n, 1]
        return re + (vr * wr - vi * wi), im + (vr * wi + vi * wr)

    zero = jnp.zeros((band, LANES), F32)
    re, im = lax.fori_loop(0, w_ref.shape[1], step, (zero, zero), unroll=4)
    out_ref[0, 0] = re
    out_ref[0, 1] = im


VM = pl.BlockSpec(memory_space=pltpu.VMEM)
SM = pl.BlockSpec(memory_space=pltpu.SMEM)


def body(fine_fields, fine_octant, mid_octant, shift_fine, shift_mid, interp_theta_mid, interp_phi_mid,
         interp_theta_top, interp_phi_top, partners, translation):
    theta_mid, theta_fine = interp_theta_mid.shape
    phi_mid, phi_fine = interp_phi_mid.shape
    theta_top, _ = interp_theta_top.shape
    phi_top, _ = interp_phi_top.shape
    dirs = lax.axis_size("dir")
    boxes = fine_fields.shape[0]
    mids = boxes // 8
    slots = mids // 8
    tops, listed, _, local = translation.shape
    band = local // phi_top
    pack = LANES // phi_fine
    per = theta_fine // pack
    rows = boxes * per

    mid_oct = lax.dynamic_slice_in_dim(mid_octant, lax.axis_index("dir") * mids, mids)
    x = fine_fields.reshape(boxes, 2, per, LANES).transpose(0, 2, 1, 3).reshape(rows * 2, LANES)
    w = translation.reshape(tops, listed, 2, band, LANES).transpose(0, 1, 3, 2, 4).reshape(
        tops, listed, 2 * band, LANES)

    cos_f = jnp.cos(shift_fine).reshape(8, theta_mid, phi_mid)
    sin_f = jnp.sin(shift_fine).reshape(8, theta_mid, phi_mid)
    cf = jnp.concatenate([cos_f, cos_f], axis=2)
    sf = jnp.concatenate([sin_f, -sin_f], axis=2)
    ct = jnp.cos(shift_mid).reshape(8, theta_top, phi_top)
    st = jnp.sin(shift_mid).reshape(8, theta_top, phi_top)

    two = jnp.eye(2, dtype=F32)
    lots = jnp.eye(pack, dtype=F32)
    wf = (two[:, None, None, None, :, None] * lots[None, :, None, :, None, None]
          * interp_phi_mid.T[None, None, :, None, None, :]).reshape(2 * LANES, pack * 2 * phi_mid)
    af = interp_theta_mid.reshape(theta_mid, per, pack).transpose(0, 2, 1).reshape(theta_mid, theta_fine)
    wt = (two[:, None, :, None] * interp_phi_top.T[None, :, None, :]).reshape(2 * phi_mid, 2 * phi_top)
    at = interp_theta_top

    params = pltpu.CompilerParams(vmem_limit_bytes=48 * 2**20)
    banded = pl.pallas_call(
        up_kernel,
        out_shape=jax.ShapeDtypeStruct((dirs, slots, 2, band, LANES), F32),
        in_specs=[SM, SM] + [VM] * 9,
        out_specs=VM,
        scratch_shapes=[
            pltpu.VMEM((pack, rows, LANES), F32),
            pltpu.VMEM((mids * theta_mid, LANES), F32),
            pltpu.VMEM((mids * theta_mid, 2 * LANES), F32),
        ],
        compiler_params=params,
        name="up",
    )(fine_octant, mid_oct, x, wf, af, wt, at, cf, sf, ct, st)

    received = lax.all_to_all(banded, "dir", split_axis=0, concat_axis=0, tiled=True)
    top_fields = received.reshape(tops, 2, band, LANES)
    portion = lax.all_gather(top_fields, "sub", axis=0, tiled=True)

    top_incoming = pl.pallas_call(
        translate_kernel,
        out_shape=jax.ShapeDtypeStruct((tops, 2, band, LANES), F32),
        grid=(tops,),
        in_specs=[
            SM,
            VM,
            pl.BlockSpec((1, listed, 2 * band, LANES), lambda t: (t, 0, 0, 0)),
        ],
        out_specs=pl.BlockSpec((1, 2, band, LANES), lambda t: (t, 0, 0, 0)),
        compiler_params=params,
        name="translate",
    )(partners, portion, w)

    parent = lax.all_to_all(
        top_incoming.reshape(dirs, slots, 2, band, LANES), "dir", split_axis=0, concat_axis=0, tiled=True)

    result = pl.pallas_call(
        down_kernel,
        out_shape=jax.ShapeDtypeStruct((rows * 2, LANES), F32),
        in_specs=[SM, SM] + [VM] * 9,
        out_specs=VM,
        scratch_shapes=[
            pltpu.VMEM((mids * theta_mid, 2 * LANES), F32),
            pltpu.VMEM((mids * theta_mid, LANES), F32),
            pltpu.VMEM((pack, rows, LANES), F32),
        ],
        compiler_params=params,
        name="down",
    )(fine_octant, mid_oct, parent, wf.T, af.T, wt.T, at.T, cf, sf, ct, st)
    return result.reshape(boxes, per, 2, LANES).transpose(0, 2, 1, 3).reshape(boxes, 2, theta_fine * phi_fine)


def solution(mesh):
    in_specs = (
        P(("sub", "dir"), None, None),
        P(("sub", "dir")),
        P("sub"),
        P(),
        P(),
        P(),
        P(),
        P(),
        P(),
        P("sub", None),
        P("sub", None, None, "dir"),
    )
    out_specs = P(("sub", "dir"), None, None)
    return jax.shard_map(body, mesh=mesh, in_specs=in_specs, out_specs=out_specs, check_vma=False)
```

profile of v0, /device:TPU:0, one launch (start us, length us, event | category | flops | bytes accessed | tf_op | source)
XLA Modules:
  0.0 142.8 jit_solution(11795219982784278392)
XLA Ops:
  6.5 0.0 copy-start.5
  6.5 0.0 copy-start.6
  6.5 0.0 all-gather.2.cloned.1.call-start
  6.6 0.8 copy.47
  7.3 0.1 copy.32.af_ref
  7.4 0.9 copy.33.at_ref
  8.3 0.1 broadcast_multiply_fusion.2
  8.4 0.9 broadcast_multiply_fusion.1
  9.2 1.4 fusion.1
  10.6 0.1 reshape.87
  10.7 0.0 copy-start.4
  10.8 0.1 reshape.86
  10.9 1.1 broadcast_multiply_fusion
  11.9 0.9 mul.62.wf_ref
  12.9 0.0 copy-done.5
  12.9 1.9 %sine_bitcast_fusion = (f32[1,8,128,128]{3,1,2,0:T(8,128)S(1)}, f32[1,8,128,128]{3,1,2,0:T(8,128)S(1)}) fusion(f32[8,16384]{1,0:T(8,128)S(1)} %copy-done.5), kind=kLoop, calls=%fused_computation.2 | loop fusion | bytes 1572864
  14.7 0.0 copy-done.6
  14.7 0.1 dynamic_slice.3.mid_oct
  14.8 0.2 pad_maximum_fusion
  15.0 0.0 copy-start.3
  15.0 0.2 copy_bitcast_fusion
  15.2 0.0 copy-done.4
  15.3 0.0 copy-start.1
  15.3 1.6 %copy-done.1 = f32[256,2,1024]{2,1,0:T(2,128)S(1)} copy-done((f32[256,2,1024]{2,1,0:T(2,128)S(1)}, f32[256,2,1024]{2,1,0:T(2,128)}, u32[]{:S(2)}) %copy-start.1) | copy-done | bytes 2097176
  16.8 12.5 %up.1 = f32[4,4,2,32,128]{4,3,2,1,0:T(8,128)S(1)} custom-call(s32[256]{0:T(256)S(1)} %copy-done.4, s32[32]{0:T(128)S(1)} %dynamic_slice.3.mid_oct, f32[4096,128]{1,0:T(8,128)S(1)} %bitcast.44, f32[256,512]{1,0:T(8,128)S(1)} %mul.62.wf_ref, f32[64,32]{1,0:T(8,128)S(1)} %copy.32.af_ref, f32[128,256]{1,0:T(8,128)S(1)} %bitcast.46, f32[128,64]{1,0:T(8,128)S(1)} %copy.33.at_ref, ...), custom_call_target="tpu_custom_call" | custom-call | tf_op jit(solution)/shard_map/up/pallas_call | solution.py:244
  29.3 20.7 %all_to_all.10 = f32[4,4,2,32,128]{4,3,2,1,0:T(8,128)} all-to-all(f32[4,4,2,32,128]{4,3,2,1,0:T(8,128)S(1)} %up.1), channel_id=1, replica_groups=mesh['sub'=8,'dir'=4] {'dir'}, dimensions={0} | all-to-all | bytes 1048576 | tf_op jit(solution)/shard_map/all_to_all | solution.py:258
  50.1 0.0 all-gather.2.cloned.1.call-update
  50.1 35.8 %all-gather.2.cloned.1.call-done.p_ref = f32[128,2,32,128]{3,2,1,0:T(8,128)} async-done(((f32[16,2,32,128]{3,2,1,0:T(8,128)}), f32[128,2,32,128]{3,2,1,0:T(8,128)}) %all-gather.2.cloned.1.call-update) | async-done | bytes 4194320 | tf_op jit(solution)/shard_map/all_gather | solution.py:260
  85.9 0.0 copy-done.3
  85.9 0.0 copy-start
  85.9 2.2 %copy-done = f32[128,2,32,128]{3,2,1,0:T(8,128)S(1)} copy-done((f32[128,2,32,128]{3,2,1,0:T(8,128)S(1)}, f32[128,2,32,128]{3,2,1,0:T(8,128)}, u32[]{:S(2)}) %copy-start) | copy-done | bytes 4194328
  88.1 0.0 copy-start.2
  88.1 13.4 %translate.1 = f32[16,2,32,128]{3,2,1,0:T(8,128)} custom-call(s32[16,32]{1,0:T(8,128)S(1)} %copy-done.3, f32[128,2,32,128]{3,2,1,0:T(8,128)S(1)} %copy-done, f32[16,32,64,128]{3,2,1,0:T(8,128)} %bitcast.52), custom_call_target="tpu_custom_call" | custom-call | tf_op jit(solution)/shard_map/translate/pallas_call | solution.py:262
  101.6 4.6 %all-to-all-start.1 = ((f32[4,4,2,32,128]{4,3,2,1,0:T(8,128)}), f32[4,4,2,32,128]{4,3,2,1,0:T(8,128)S(1)}, u32[]{:S(2)}, u32[]{:S(2)}) async-start(f32[4,4,2,32,128]{4,3,2,1,0:T(8,128)} %bitcast.12), calls=%async_computation.1 | async-start | bytes 1048576 | tf_op jit(solution)/shard_map/all_to_all | solution.py:276
  106.2 0.1 copy.36
  106.2 0.2 copy.35
  106.5 14.6 %all-to-all-done.1.r_ref = f32[4,4,2,32,128]{4,3,2,1,0:T(8,128)S(1)} async-done(((f32[4,4,2,32,128]{4,3,2,1,0:T(8,128)}), f32[4,4,2,32,128]{4,3,2,1,0:T(8,128)S(1)}, u32[]{:S(2)}, u32[]{:S(2)}) %all-to-all-start.1) | async-done | bytes 524320 | tf_op jit(solution)/shard_map/all_to_all | solution.py:276
  121.1 0.0 copy-done.2
  121.1 14.9 %down.1 = f32[4096,128]{1,0:T(8,128)} custom-call(s32[256]{0:T(256)S(1)} %copy-done.4, s32[32]{0:T(128)S(1)} %dynamic_slice.3.mid_oct, f32[4,4,2,32,128]{4,3,2,1,0:T(8,128)S(1)} %all-to-all-done.1.r_ref, f32[512,256]{1,0:T(8,128)S(1)} %bitcast.45, f32[32,64]{1,0:T(8,128)S(1)} %bitcast.50, f32[256,128]{1,0:T(8,128)S(1)} %bitcast.48, f32[64,128]{1,0:T(8,128)S(1)} %bitcast.51, ...), custom_call_target="tpu_custom_call" | custom-call | tf_op jit(solution)/shard_map/down/pallas_call | solution.py:279
  (4 shorter events, 0.0 us)
Async XLA Ops:
  6.5 6.3 %copy-start.5 = (f32[8,16384]{1,0:T(8,128)S(1)}, f32[8,16384]{1,0:T(8,128)}, u32[]{:S(2)}) copy-start(f32[8,16384]{1,0:T(8,128)} %param.15) | copy-start | bytes 1572868
  6.5 8.2 %copy-start.6 = (s32[128]{0:T(128)S(1)}, s32[128]{0:T(128)}, u32[]{:S(2)}) copy-start(s32[128]{0:T(128)} %param.13) | copy-start | bytes 1540
  6.5 79.4 %all-gather.2.cloned.1.call-start = ((), (), s32[]{:S(2)}) async-start(), calls=%async_computation.2 | async-start | bytes 4718592 | tf_op jit(solution)/shard_map/all_gather | solution.py:260
  10.7 4.5 %copy-start.4 = (s32[256]{0:T(256)S(1)}, s32[256]{0:T(256)}, u32[]{:S(2)}) copy-start(s32[256]{0:T(256)} %fine_oct.3) | copy-start | bytes 3076
  15.0 70.9 %copy-start.3 = (s32[16,32]{1,0:T(8,128)S(1)}, s32[16,32]{1,0:T(8,128)}, u32[]{:S(2)}) copy-start(s32[16,32]{1,0:T(8,128)} %partners.1) | copy-start | bytes 6148
  15.3 1.6 %copy-start.1 = (f32[256,2,1024]{2,1,0:T(2,128)S(1)}, f32[256,2,1024]{2,1,0:T(2,128)}, u32[]{:S(2)}) copy-start(f32[256,2,1024]{2,1,0:T(2,128)} %param.11) | copy-start | bytes 6291460
  85.9 2.2 %copy-start = (f32[128,2,32,128]{3,2,1,0:T(8,128)S(1)}, f32[128,2,32,128]{3,2,1,0:T(8,128)}, u32[]{:S(2)}) copy-start(f32[128,2,32,128]{3,2,1,0:T(8,128)} %all-gather.2.cloned.1.call-done.p_ref) | copy-start | bytes 12582916
  88.1 32.9 %copy-start.2 = (f32[128,64]{0,1:T(8,128)S(1)}, f32[128,64]{0,1:T(8,128)}, u32[]{:S(2)}) copy-start(f32[128,64]{0,1:T(8,128)} %param.18) | copy-start | bytes 98308
  101.6 19.5 %all-to-all-start.1 = ((f32[4,4,2,32,128]{4,3,2,1,0:T(8,128)}), f32[4,4,2,32,128]{4,3,2,1,0:T(8,128)S(1)}, u32[]{:S(2)}, u32[]{:S(2)}) async-start(f32[4,4,2,32,128]{4,3,2,1,0:T(8,128)} %bitcast.12), calls=%async_computation.1 | async-start | bytes 1048576 | tf_op jit(solution)/shard_map/all_to_all | solution.py:276
Sparse Core Ops, SparseCore 0:
  50.2 35.6 all-gather.1
where the time goes:
time: 144 us; the launch traced here: 143 us
  waiting for transfers between devices  50.5 us (35%)
  Pallas kernels  40.8 us (28%)
  blocking collectives  20.7 us (14%)
  between operations  13.5 us (9%)
  local copies, waits for them, and re-layouts  10.4 us (7%)
  starting transfers between devices  4.6 us (3%)
  other arithmetic  2.23 us (2%)
    all_gather x1, waiting for transfers between devices, body(): portion = lax.all_gather(top_fields, 'sub', axis=0, tiled=True)  35.8 us
    all_to_all x1, blocking collectives, body(): lax.all_to_all(banded, 'dir', split_axis=0, concat_axis=0, tiled=True)  20.7 us
    pallas_call x1, Pallas kernels, body(): pl.pallas_call(down_kernel, out_shape=jax.ShapeDtypeStruct((rows * 2, LAN...  14.9 us
    all_to_all x1, waiting for transfers between devices, body(): lax.all_to_all(top_incoming.reshape(dirs, slots, 2, band, LANES), 'dir',...  14.6 us
    pallas_call x1, Pallas kernels, body(): pl.pallas_call(translate_kernel, out_shape=jax.ShapeDtypeStruct((tops, 2,...  13.4 us
    pallas_call x1, Pallas kernels, body(): pl.pallas_call(up_kernel, out_shape=jax.ShapeDtypeStruct((dirs, slots, 2,...  12.5 us
    unnamed x17, local copies, waits for them, and re-layouts  6.51 us
    all_to_all x1, starting transfers between devices, body(): lax.all_to_all(top_incoming.reshape(dirs, slots, 2, band, LANES), 'dir',...  4.6 us
  transfers between devices with their start and end apart: 2, of which 2 were waited for; matrix products, arithmetic and copies ran while one was open for 0% of the time, Pallas kernels for 0%

commit v1 on v0

--- a/solution.py
+++ b/solution.py
@@ -1,5 +1,3 @@
-import functools
-
 import jax
 import jax.numpy as jnp
 from jax import lax
@@ -8,6 +6,8 @@
 from jax.sharding import PartitionSpec as P
 
 LANES = 128
+PIECES = 4
+MESH = pl.DeviceIdType.MESH
 BF = jnp.bfloat16
 F32 = jnp.float32
 
@@ -182,26 +182,149 @@
         out_ref[pl.ds(2 * base + 1, step, stride=2), :] = y[:, LANES:]
 
 
-def translate_kernel(partners, p_ref, w_ref, out_ref):
-    t = pl.program_id(0)
-    band = p_ref.shape[2]
-
-    def step(k, carry):
-        re, im = carry
-        n = partners[t, k]
-        wr = w_ref[0, k, pl.ds(0, band, stride=2), :]
-        wi = w_ref[0, k, pl.ds(1, band, stride=2), :]
-        vr, vi = p_ref[n, 0], p_ref[n, 1]
-        return re + (vr * wr - vi * wi), im + (vr * wi + vi * wr)
-
-    zero = jnp.zeros((band, LANES), F32)
-    re, im = lax.fori_loop(0, w_ref.shape[1], step, (zero, zero), unroll=4)
-    out_ref[0, 0] = re
-    out_ref[0, 1] = im
+def exchange_kernel(partners, banded_ref, w_hbm, out_ref, p_ref, w_ref, o_ref,
+                    w_sem, own_sem, a_send, a_recv, cw_send, cw_recv, ccw_send, ccw_recv,
+                    part_send, part_recv, r_send, r_recv):
+    dirs, slots, _, band, _ = banded_ref.shape
+    tops, listed = w_ref.shape[:2]
+    subs = p_ref.shape[0] // tops
+    chips = subs // 2
+    wide = chips // 2
+    hops = chips // 2
+    group = dirs // PIECES
+    many = group * slots
+
+    me = lax.axis_index("sub")
+    z = lax.axis_index("dir")
+    core = lax.rem(me, 2)
+
+    def flip(c):
+        return jnp.where(c < wide, c, 3 * wide - 1 - c)
+
+    ring = flip(me // 2)
+
+    def at_ring(step):
+        return 2 * flip(lax.rem(ring + step + chips, chips)) + core
+
+    right, left = at_ring(1), at_ring(-1)
+    partner = me + 1 - 2 * core
+    peers = [lax.rem(z + e, dirs) for e in range(1, dirs)]
+
+    barrier = pltpu.get_barrier_semaphore()
+    for d in peers:
+        pl.semaphore_signal(barrier, inc=1, device_id=(me, d), device_id_type=MESH)
+    for s in (right, left, partner):
+        pl.semaphore_signal(barrier, inc=1, device_id=(s, z), device_id_type=MESH)
+    pl.semaphore_wait(barrier, dirs + 2)
+
+    def push(src, dst, send, recv, device):
+        return pltpu.make_async_remote_copy(
+            src_ref=src, dst_ref=dst, send_sem=send, recv_sem=recv, device_id=device, device_id_type=MESH)
+
+    def block(source):
+        return p_ref.at[pl.ds(me * tops + source * slots, slots)]
+
+    own = pltpu.make_async_copy(banded_ref.at[z], block(z), own_sem)
+    own.start()
+    first = []
+    for e in range(1, dirs):
+        d = lax.rem(z - e + dirs, dirs)
+        copy = push(banded_ref.at[d], block(z), a_send.at[e], a_recv.at[e], (me, d))
+        copy.start()
+        first.append(copy)
+    loads = []
+    for t in range(tops):
+        copy = pltpu.make_async_copy(w_hbm.at[t], w_ref.at[t], w_sem.at[t])
+        copy.start()
+        loads.append(copy)
+
+    def piece(sub, i):
+        g = lax.rem(z // group + i, PIECES)
+        return p_ref.at[pl.ds(sub * tops + g * many, many)]
+
+    sent, handed = [], []
+
+    def ship(view, send, recv, device, keep):
+        copy = push(view, view, send, recv, device)
+        copy.start()
+        keep.append(copy)
+
+    own.wait()
+    arrived = 0
+    for step in range(PIECES + hops):
+        if step < PIECES:
+            last = dirs - 1 if step == PIECES - 1 or group > 1 else step
+            while arrived < last:
+                first[arrived].wait_recv()
+                arrived += 1
+            view = piece(me, step)
+            ship(view, cw_send.at[0, step], cw_recv.at[0, step], (right, z), sent)
+            ship(view, ccw_send.at[0, step], ccw_recv.at[0, step], (left, z), sent)
+            ship(view, part_send.at[0, step], part_recv.at[0, step], (partner, z), handed)
+        for h in range(1, hops + 1):
+            i = step - h
+            if not 0 <= i < PIECES:
+                continue
+            for way in range(2):
+                forward = i < PIECES // 2 if way == 0 else i >= PIECES // 2
+                if h == hops and not forward:
+                    continue
+                send, recv = (cw_send, cw_recv) if way == 0 else (ccw_send, ccw_recv)
+                target = right if way == 0 else left
+                view = piece(at_ring(-h if way == 0 else h), i)
+                push(view, view, send.at[h - 1, i], recv.at[h - 1, i], (target, z)).wait_recv()
+                if h + 1 < hops or (h + 1 == hops and forward):
+                    ship(view, send.at[h, i], recv.at[h, i], (target, z), sent)
+                slot = 2 * h - 1 + way
+                ship(view, part_send.at[slot, i], part_recv.at[slot, i], (partner, z), handed)
+    for copy in handed:
+        copy.wait_recv()
+    for copy in loads:
+        copy.wait()
+
+    def translate(t):
+        def one(k, carry):
+            re, im = carry
+            n = partners[t, k]
+            wr = w_ref[t, k, pl.ds(0, band, stride=2), :]
+            wi = w_ref[t, k, pl.ds(1, band, stride=2), :]
+            vr, vi = p_ref[n, 0], p_ref[n, 1]
+            return re + (vr * wr - vi * wi), im + (vr * wi + vi * wr)
+
+        zero = jnp.zeros((band, LANES), F32)
+        re, im = lax.fori_loop(0, listed, one, (zero, zero), unroll=4)
+        o_ref[t, 0] = re
+        o_ref[t, 1] = im
+
+    returns = []
+    waiting = None
+    for e in range(1, dirs + 1):
+        d = lax.rem(z + e, dirs)
+        translate(d * slots)
+        if waiting is not None:
+            waiting.start()
+            returns.append(waiting)
+            waiting = None
+        if slots > 1:
+            def more(q, carry, d=d):
+                translate(d * slots + q)
+                return carry
+
+            lax.fori_loop(1, slots, more, 0)
+        if e < dirs:
+            waiting = push(o_ref.at[pl.ds(d * slots, slots)], out_ref.at[z], r_send.at[e], r_recv.at[e], (me, d))
+    for copy in returns:
+        copy.wait()
+    own = pltpu.make_async_copy(o_ref.at[pl.ds(z * slots, slots)], out_ref.at[z], own_sem)
+    own.start()
+    for copy in first + sent + handed:
+        copy.wait_send()
+    own.wait()
 
 
 VM = pl.BlockSpec(memory_space=pltpu.VMEM)
 SM = pl.BlockSpec(memory_space=pltpu.SMEM)
+ANY = pl.BlockSpec(memory_space=pl.ANY)
 
 
 def body(fine_fields, fine_octant, mid_octant, shift_fine, shift_mid, interp_theta_mid, interp_phi_mid,
@@ -255,26 +378,35 @@
         name="up",
     )(fine_octant, mid_oct, x, wf, af, wt, at, cf, sf, ct, st)
 
-    received = lax.all_to_all(banded, "dir", split_axis=0, concat_axis=0, tiled=True)
-    top_fields = received.reshape(tops, 2, band, LANES)
-    portion = lax.all_gather(top_fields, "sub", axis=0, tiled=True)
-
-    top_incoming = pl.pallas_call(
-        translate_kernel,
-        out_shape=jax.ShapeDtypeStruct((tops, 2, band, LANES), F32),
-        grid=(tops,),
-        in_specs=[
-            SM,
-            VM,
-            pl.BlockSpec((1, listed, 2 * band, LANES), lambda t: (t, 0, 0, 0)),
+    subs = lax.axis_size("sub")
+    hops = subs // 4
+    dma = pltpu.SemaphoreType.DMA
+    parent = pl.pallas_call(
+        exchange_kernel,
+        out_shape=jax.ShapeDtypeStruct((dirs, slots, 2, band, LANES), F32),
+        in_specs=[SM, ANY, ANY],
+        out_specs=ANY,
+        scratch_shapes=[
+            pltpu.VMEM((subs * tops, 2, band, LANES), F32),
+            pltpu.VMEM((tops, listed, 2 * band, LANES), F32),
+            pltpu.VMEM((tops, 2, band, LANES), F32),
+            dma((tops,)),
+            dma,
+            dma((dirs,)),
+            dma((dirs,)),
+            dma((hops, PIECES)),
+            dma((hops, PIECES)),
+            dma((hops, PIECES)),
+            dma((hops, PIECES)),
+            dma((2 * hops + 1, PIECES)),
+            dma((2 * hops + 1, PIECES)),
+            dma((dirs,)),
+            dma((dirs,)),
         ],
-        out_specs=pl.BlockSpec((1, 2, band, LANES), lambda t: (t, 0, 0, 0)),
-        compiler_params=params,
-        name="translate",
-    )(partners, portion, w)
-
-    parent = lax.all_to_all(
-        top_incoming.reshape(dirs, slots, 2, band, LANES), "dir", split_axis=0, concat_axis=0, tiled=True)
+        compiler_params=pltpu.CompilerParams(
+            vmem_limit_bytes=48 * 2**20, collective_id=0, has_side_effects=True),
+        name="exchange",
+    )(partners, banded, w)
 
     result = pl.pallas_call(
         down_kernel,

time: 144 us -> 80.3 us (0.56)
  waiting for transfers between devices: 50.5 us -> 0 us
  Pallas kernels: 40.8 us -> 69.7 us
  blocking collectives: 20.7 us -> 0 us
  between operations: 13.5 us -> 0.18 us
  starting transfers between devices: 4.6 us -> 0 us
  local copies, waits for them, and re-layouts: 10.4 us -> 7.65 us
    all_gather x1 -> x0, waiting for transfers between devices: 35.8 us -> none  [body(): portion = lax.all_gather(top_fields, 'sub', axis=0, tiled=True)]
    pallas_call x1, Pallas kernels: 13.4 us -> 42.5 us  [body(): pl.pallas_call(exchange_kernel, out_shape=jax.ShapeDtypeStruct((dirs, slo...]
    all_to_all x1 -> x0, blocking collectives: 20.7 us -> none  [body(): lax.all_to_all(banded, 'dir', split_axis=0, concat_axis=0, tiled=True)]
    all_to_all x1 -> x0, waiting for transfers between devices: 14.6 us -> none  [body(): lax.all_to_all(top_incoming.reshape(dirs, slots, 2, band, LANES), 'dir',...]
    all_to_all x1 -> x0, starting transfers between devices: 4.6 us -> none  [body(): lax.all_to_all(top_incoming.reshape(dirs, slots, 2, band, LANES), 'dir',...]
    unnamed x17 -> x15, local copies, waits for them, and re-layouts: 6.51 us -> 3.11 us
  transfers between devices with their start and end apart: 2 -> 0, of which waited for: 2 -> 0; matrix products, arithmetic and copies ran while one was open for 0% -> 0% of each run, Pallas kernels for 0% -> 0%
where the time goes in v1:
time: 80.3 us; the launch traced here: 79 us
  Pallas kernels  69.7 us (87%)
  local copies, waits for them, and re-layouts  7.65 us (10%)
  other arithmetic  1.51 us (2%)
    pallas_call x1, Pallas kernels, body(): pl.pallas_call(exchange_kernel, out_shape=jax.ShapeDtypeStruct((dirs, slo...  42.5 us
    pallas_call x1, Pallas kernels, body(): pl.pallas_call(down_kernel, out_shape=jax.ShapeDtypeStruct((rows * 2, LAN...  14.7 us
    pallas_call x1, Pallas kernels, body(): pl.pallas_call(up_kernel, out_shape=jax.ShapeDtypeStruct((dirs, slots, 2,...  12.4 us
    unnamed x15, local copies, waits for them, and re-layouts  3.11 us

profile of v1, /device:TPU:0, one launch (start us, length us, event | category | flops | bytes accessed | tf_op | source)
XLA Modules:
  0.0 79.0 jit_solution(11978984626514315058)
XLA Ops:
  0.0 0.7 dynamic_slice.3.mid_oct
  0.7 0.1 broadcast_multiply_fusion.2
  0.8 0.7 copy.39
  1.5 0.1 copy.24.af_ref
  1.6 0.9 %copy.25.at_ref = f32[128,64]{1,0:T(8,128)S(1)} copy(f32[128,64]{0,1:T(8,128)} %param.18) | data formatting | bytes 65536 | tf_op args[7]
  2.5 0.9 %broadcast_multiply_fusion.1 = f32[2,64,2,128]{3,2,1,0:T(2,128)S(1)} fusion(f32[64,128]{1,0:T(8,128)} %bitcast.52, f32[2,2]{1,0:T(2,128)S(1)} %compare_convert_fusion), kind=kLoop, calls=%fused_computation.8 | loop fusion | flops 32768 | bytes 163856 | tf_op jit(solution)/shard_map/mul | solution.py:363
  3.4 0.1 copy.28
  3.5 1.4 %fusion.1 = (f32[8,4096]{1,0:T(8,128)S(1)}, f32[8,4096]{1,0:T(8,128)S(1)}) fusion(f32[8,4096]{1,0:T(8,128)} %param.14), kind=kLoop, calls=%fused_computation.15 | loop fusion | bytes 393216 | tf_op jit(solution)/shard_map/sin | solution.py:352
  4.8 0.1 reshape.81
  4.9 0.0 copy-start.5
  5.0 0.1 reshape.80
  5.1 0.2 pad_maximum_fusion
  5.3 0.0 copy-start.4
  5.3 0.4 copy-done.5
  5.7 0.3 broadcast_multiply_fusion
  6.0 0.9 %mul.62.wf_ref = f32[256,512]{1,0:T(8,128)S(1)} reshape(f32[2,4,32,4,2,64]{5,4,3,2,1,0:T(2,128)S(1)} %broadcast_multiply_fusion) | data formatting | bytes 1048576 | tf_op jit(solution)/shard_map/mul | solution.py:360
  6.9 0.2 copy.27
  7.1 0.0 copy-start
  7.2 0.0 copy-start.3
  7.2 0.0 copy-done.4
  7.2 1.9 %sine_bitcast_fusion = (f32[1,8,128,128]{3,1,2,0:T(8,128)S(1)}, f32[1,8,128,128]{3,1,2,0:T(8,128)S(1)}) fusion(f32[8,16384]{1,0:T(8,128)S(1)} %copy-done.4), kind=kLoop, calls=%fused_computation.2 | loop fusion | bytes 1572864
  9.0 0.2 copy_bitcast_fusion
  9.3 0.0 copy-done
  9.3 0.0 copy-done.3
  9.3 0.0 copy-start.2
  9.3 12.4 %up.1.banded_ref = f32[4,4,2,32,128]{4,3,2,1,0:T(8,128)S(1)} custom-call(s32[256]{0:T(256)S(1)} %copy-done.3, s32[32]{0:T(128)S(1)} %dynamic_slice.3.mid_oct, f32[4096,128]{1,0:T(8,128)S(1)} %bitcast.42, f32[256,512]{1,0:T(8,128)S(1)} %mul.62.wf_ref, f32[64,32]{1,0:T(8,128)S(1)} %copy.24.af_ref, f32[128,256]{1,0:T(8,128)S(1)} %bitcast.45, ...), custom_call_target="tpu_custom_call" | custom-call | tf_op jit(solution)/shard_map/up/pallas_call | solution.py:367
  21.7 0.0 copy-done.2
  21.7 0.0 copy-start.1
  21.7 42.5 %exchange.1.r_ref = f32[4,4,2,32,128]{4,3,2,1,0:T(8,128)S(1)} custom-call(s32[16,32]{1,0:T(8,128)S(1)} %copy-done.2, f32[4,4,2,32,128]{4,3,2,1,0:T(8,128)S(1)} %up.1.banded_ref, f32[16,32,64,128]{3,2,1,0:T(8,128)} %bitcast.50), custom_call_target="tpu_custom_call" | custom-call | tf_op jit(solution)/shard_map/exchange/pallas_call | solution.py:384
  64.3 0.0 copy-done.1
  64.3 14.7 %down.1 = f32[4096,128]{1,0:T(8,128)} custom-call(s32[256]{0:T(256)S(1)} %copy-done.3, s32[32]{0:T(128)S(1)} %dynamic_slice.3.mid_oct, f32[4,4,2,32,128]{4,3,2,1,0:T(8,128)S(1)} %exchange.1.r_ref, f32[512,256]{1,0:T(8,128)S(1)} %bitcast.43, f32[32,64]{1,0:T(8,128)S(1)} %bitcast.48, f32[256,128]{1,0:T(8,128)S(1)} %bitcast.46, f32[64,128]{1,0:T(8,128)S(1)} %bitcast.49, ...), custom_call_target="tpu_custom_call" | custom-call | tf_op jit(solution)/shard_map/down/pallas_call | solution.py:411
  (4 shorter events, 0.0 us)
Async XLA Ops:
  4.9 0.7 copy-start.5
  5.3 1.9 %copy-start.4 = (f32[8,16384]{1,0:T(8,128)S(1)}, f32[8,16384]{1,0:T(8,128)}, u32[]{:S(2)}) copy-start(f32[8,16384]{1,0:T(8,128)} %param.15) | copy-start | bytes 1572868
  7.1 2.1 %copy-start = (f32[256,2,1024]{2,1,0:T(2,128)S(1)}, f32[256,2,1024]{2,1,0:T(2,128)}, u32[]{:S(2)}) copy-start(f32[256,2,1024]{2,1,0:T(2,128)} %param.11) | copy-start | bytes 6291460
  7.2 2.1 %copy-start.3 = (s32[256]{0:T(256)S(1)}, s32[256]{0:T(256)}, u32[]{:S(2)}) copy-start(s32[256]{0:T(256)} %fine_oct.3) | copy-start | bytes 3076
  9.3 12.4 %copy-start.2 = (s32[16,32]{1,0:T(8,128)S(1)}, s32[16,32]{1,0:T(8,128)}, u32[]{:S(2)}) copy-start(s32[16,32]{1,0:T(8,128)} %partners.1) | copy-start | bytes 6148
  21.7 42.6 %copy-start.1 = (f32[128,64]{0,1:T(8,128)S(1)}, f32[128,64]{0,1:T(8,128)}, u32[]{:S(2)}) copy-start(f32[128,64]{0,1:T(8,128)} %param.18) | copy-start | bytes 98308

commit v2 on v0

--- a/solution.py
+++ b/solution.py
@@ -1,5 +1,3 @@
-import functools
-
 import jax
 import jax.numpy as jnp
 from jax import lax
@@ -8,6 +6,7 @@
 from jax.sharding import PartitionSpec as P
 
 LANES = 128
+MESH = pl.DeviceIdType.MESH
 BF = jnp.bfloat16
 F32 = jnp.float32
 
@@ -40,77 +39,221 @@
     return min(rows, 512)
 
 
-def up_kernel(fine_oct, mid_oct, x_ref, wf_ref, af_ref, wt_ref, at_ref, cf_ref, sf_ref, ct_ref, st_ref,
-              out_ref, y_ref, mid_ref, z_ref):
-    pack = y_ref.shape[0]
-    rows = y_ref.shape[1]
+def up_kernel(fine_oct, mid_oct, partners, x_ref, wf_ref, af_ref, wt_ref, at_ref, cf_ref, sf_ref, ct_ref, st_ref,
+              w_hbm, out_ref, y_ref, mid_ref, z_ref, banded_ref, p_ref, w_ref, o_ref,
+              w_sem, own_sem, last_sem, a_send, a_recv, cw_send, cw_recv, ccw_send, ccw_recv,
+              part_send, part_recv, r_send, r_recv):
+    pack, step, _ = y_ref.shape
     theta_mid = cf_ref.shape[1]
     theta_fine = af_ref.shape[1]
     per = theta_fine // pack
-    theta_top = ct_ref.shape[1]
-    mids = mid_ref.shape[0] // theta_mid
-    dirs, slots, _, band, _ = out_ref.shape
     half = LANES // 2
+    dirs, slots, _, band, _ = banded_ref.shape
+    tops, listed = w_ref.shape[:2]
+    subs = p_ref.shape[0] // tops
+    chips = subs // 2
+    wide = chips // 2
+    hops = chips // 2
+
+    me = lax.axis_index("sub")
+    z = lax.axis_index("dir")
+    core = lax.rem(me, 2)
+
+    def flip(c):
+        return jnp.where(c < wide, c, 3 * wide - 1 - c)
+
+    ring = flip(me // 2)
+
+    def at_ring(move):
+        return 2 * flip(lax.rem(ring + move + chips, chips)) + core
+
+    right, left = at_ring(1), at_ring(-1)
+    partner = me + 1 - 2 * core
+
+    barrier = pltpu.get_barrier_semaphore()
+    for e in range(1, dirs):
+        pl.semaphore_signal(barrier, inc=1, device_id=(me, lax.rem(z + e, dirs)), device_id_type=MESH)
+    for s in (right, left, partner):
+        pl.semaphore_signal(barrier, inc=1, device_id=(s, z), device_id_type=MESH)
+    loads = []
+    for t in range(tops):
+        copy = pltpu.make_async_copy(w_hbm.at[t], w_ref.at[t], w_sem.at[t])
+        copy.start()
+        loads.append(copy)
+    pl.semaphore_wait(barrier, dirs + 2)
+
+    def push(src, dst, send, recv, device):
+        return pltpu.make_async_remote_copy(
+            src_ref=src, dst_ref=dst, send_sem=send, recv_sem=recv, device_id=device, device_id_type=MESH)
+
+    def spread(q):
+        dst = p_ref.at[me * tops + q * dirs + z]
+        copies = []
+        for e in range(1, dirs):
+            d = lax.rem(z - e + dirs, dirs)
+            copies.append(push(banded_ref.at[d, q], dst, a_send.at[e, q], a_recv.at[e, q], (me, d)))
+        return copies, pltpu.make_async_copy(banded_ref.at[z, q], dst, own_sem.at[q])
+
+    def start_spread(q):
+        copies, own = spread(q)
+        for copy in copies:
+            copy.start()
+        own.start()
+
+    def piece(sub, i):
+        return p_ref.at[pl.ds(sub * tops + i * dirs, dirs)]
+
+    def own_copies(q):
+        view = piece(me, q)
+        return [
+            push(view, view, cw_send.at[0, q], cw_recv.at[0, q], (right, z)),
+            push(view, view, ccw_send.at[0, q], ccw_recv.at[0, q], (left, z)),
+            push(view, view, part_send.at[0, q], part_recv.at[0, q], (partner, z)),
+        ]
+
+    def own_ship(q):
+        copies, own = spread(q)
+        for copy in copies:
+            copy.wait_recv()
+        own.wait()
+        for copy in own_copies(q):
+            copy.start()
 
     wf_hi, wf_lo = split(wf_ref[...])
-    step = chunk_of(rows)
-
-    @pl.loop(0, rows // step)
-    def _(i):
-        base = pl.multiple_of(i * step, 8)
+    wt_hi, wt_lo = split(wt_ref[...])
+    a_mid = left3(af_ref[...])
+    a_top = left3(at_ref[...])
+    banded_ref[...] = jnp.zeros_like(banded_ref)
+
+    @pl.loop(0, slots)
+    def _(q):
+        base = pl.multiple_of(q * step, 8)
         re = x_ref[pl.ds(2 * base, step, stride=2), :]
         im = x_ref[pl.ds(2 * base + 1, step, stride=2), :]
         y = wide_dot(jnp.concatenate([re, im], axis=1), wf_hi, wf_lo)
         for a in range(pack):
-            y_ref[a, pl.ds(base, step), :] = y[:, a * LANES:(a + 1) * LANES]
-
-    a_mid = left3(af_ref[...])
-
-    def box(b):
-        start = pl.multiple_of(b * per, per)
-        return jnp.concatenate([y_ref[a, pl.ds(start, per), :] for a in range(pack)], axis=0)
-
-    def mid_step(m, carry):
-        acc1 = jnp.zeros((theta_mid, LANES), F32)
-        acc2 = jnp.zeros((theta_mid, LANES), F32)
-        for i in range(0, 8, 2):
-            b = m * 8 + i
-            z = mm(a_mid, right3(jnp.concatenate([box(b), box(b + 1)], axis=1)))
-            for side in range(2):
-                o = fine_oct[b + side]
-                part = z[:, side * LANES:(side + 1) * LANES]
-                acc1 += part * cf_ref[o]
-                acc2 += part * sf_ref[o]
-        mid_ref[pl.ds(pl.multiple_of(m * theta_mid, theta_mid), theta_mid), :] = acc1 + pltpu.roll(acc2, half, 1)
-        return carry
-
-    lax.fori_loop(0, mids, mid_step, 0, unroll=2)
-
-    wt_hi, wt_lo = split(wt_ref[...])
-    mid_rows = mids * theta_mid
-    step2 = chunk_of(mid_rows)
-
-    @pl.loop(0, mid_rows // step2)
-    def _(i):
-        base = pl.multiple_of(i * step2, 8)
-        z_ref[pl.ds(base, step2), :] = wide_dot(mid_ref[pl.ds(base, step2), :], wt_hi, wt_lo)
-
-    a_top = left3(at_ref[...])
-    out_ref[...] = jnp.zeros_like(out_ref)
-
-    def top_step(m, carry):
-        q = m // 8
-        o = mid_oct[m]
-        z = mm(a_top, right3(z_ref[pl.ds(pl.multiple_of(m * theta_mid, theta_mid), theta_mid), :]))
-        for d in range(dirs):
-            at = slice(d * band, (d + 1) * band)
-            c, s = ct_ref[o, at, :], st_ref[o, at, :]
-            re, im = z[at, :LANES], z[at, LANES:]
-            out_ref[d, q, 0] += re * c - im * s
-            out_ref[d, q, 1] += re * s + im * c
-        return carry
-
-    lax.fori_loop(0, mids, top_step, 0, unroll=2)
+            y_ref[a] = y[:, a * LANES:(a + 1) * LANES]
+
+        @pl.when(q > 0)
+        def _():
+            start_spread(q - 1)
+
+        @pl.when(q > 1)
+        def _():
+            own_ship(q - 2)
+
+        def box(b):
+            start = pl.multiple_of(b * per, per)
+            return jnp.concatenate([y_ref[a, pl.ds(start, per), :] for a in range(pack)], axis=0)
+
+        def mid_step(m, carry):
+            acc1 = jnp.zeros((theta_mid, LANES), F32)
+            acc2 = jnp.zeros((theta_mid, LANES), F32)
+            for i in range(0, 8, 2):
+                b = m * 8 + i
+                v = mm(a_mid, right3(jnp.concatenate([box(b), box(b + 1)], axis=1)))
+                for side in range(2):
+                    o = fine_oct[q * 64 + b + side]
+                    part = v[:, side * LANES:(side + 1) * LANES]
+                    acc1 += part * cf_ref[o]
+                    acc2 += part * sf_ref[o]
+            mid_ref[pl.ds(pl.multiple_of(m * theta_mid, theta_mid), theta_mid), :] = acc1 + pltpu.roll(acc2, half, 1)
+            return carry
+
+        lax.fori_loop(0, 8, mid_step, 0, unroll=2)
+        z_ref[...] = wide_dot(mid_ref[...], wt_hi, wt_lo)
+
+        def top_step(m, carry):
+            o = mid_oct[q * 8 + m]
+            v = mm(a_top, right3(z_ref[pl.ds(pl.multiple_of(m * theta_mid, theta_mid), theta_mid), :]))
+            for d in range(dirs):
+                at = slice(d * band, (d + 1) * band)
+                c, s = ct_ref[o, at, :], st_ref[o, at, :]
+                re, im = v[at, :LANES], v[at, LANES:]
+                banded_ref[d, q, 0] += re * c - im * s
+                banded_ref[d, q, 1] += re * s + im * c
+            return carry
+
+        lax.fori_loop(0, 8, top_step, 0, unroll=2)
+
+    if slots > 1:
+        own_ship(slots - 2)
+    start_spread(slots - 1)
+
+    sent, handed = [], []
+
+    def ship(view, send, recv, device, keep):
+        copy = push(view, view, send, recv, device)
+        copy.start()
+        keep.append(copy)
+
+    for turn in range(1, slots + hops):
+        if turn == min(slots, 2):
+            own_ship(slots - 1)
+        for h in range(1, hops + 1):
+            i = turn - h
+            if not 0 <= i < slots:
+                continue
+            for way in range(2):
+                forward = i < slots // 2 if way == 0 else i >= slots // 2
+                if h == hops and not forward:
+                    continue
+                send, recv = (cw_send, cw_recv) if way == 0 else (ccw_send, ccw_recv)
+                target = right if way == 0 else left
+                view = piece(at_ring(-h if way == 0 else h), i)
+                push(view, view, send.at[h - 1, i], recv.at[h - 1, i], (target, z)).wait_recv()
+                if h + 1 < hops or (h + 1 == hops and forward):
+                    ship(view, send.at[h, i], recv.at[h, i], (target, z), sent)
+                slot = 2 * h - 1 + way
+                ship(view, part_send.at[slot, i], part_recv.at[slot, i], (partner, z), handed)
+    for q in range(slots):
+        own_copies(q)[2].wait_recv()
+    for copy in handed:
+        copy.wait_recv()
+    for copy in loads:
+        copy.wait()
+
+    def translate(t):
+        def one(k, carry):
+            re, im = carry
+            n = partners[t, k]
+            wr = w_ref[t, k, pl.ds(0, band, stride=2), :]
+            wi = w_ref[t, k, pl.ds(1, band, stride=2), :]
+            vr, vi = p_ref[n, 0], p_ref[n, 1]
+            return re + (vr * wr - vi * wi), im + (vr * wi + vi * wr)
+
+        zero = jnp.zeros((band, LANES), F32)
+        re, im = lax.fori_loop(0, listed, one, (zero, zero), unroll=4)
+        o_ref[t, 0] = re
+        o_ref[t, 1] = im
+
+    returns = []
+    waiting = None
+    for e in range(1, dirs + 1):
+        d = lax.rem(z + e, dirs)
+        translate(d * slots)
+        if waiting is not None:
+            waiting.start()
+            returns.append(waiting)
+            waiting = None
+        if slots > 1:
+            def more(q, carry, d=d):
+                translate(d * slots + q)
+                return carry
+
+            lax.fori_loop(1, slots, more, 0)
+        if e < dirs:
+            waiting = push(o_ref.at[pl.ds(d * slots, slots)], out_ref.at[z], r_send.at[e], r_recv.at[e], (me, d))
+    for copy in returns:
+        copy.wait()
+    own = pltpu.make_async_copy(o_ref.at[pl.ds(z * slots, slots)], out_ref.at[z], last_sem)
+    own.start()
+    for q in range(slots):
+        for copy in spread(q)[0] + own_copies(q):
+            copy.wait_send()
+    for copy in sent + handed:
+        copy.wait_send()
+    own.wait()
 
 
 def down_kernel(fine_oct, mid_oct, r_ref, wf_ref, af_ref, wt_ref, at_ref, cf_ref, sf_ref, ct_ref, st_ref,
@@ -182,26 +325,9 @@
         out_ref[pl.ds(2 * base + 1, step, stride=2), :] = y[:, LANES:]
 
 
-def translate_kernel(partners, p_ref, w_ref, out_ref):
-    t = pl.program_id(0)
-    band = p_ref.shape[2]
-
-    def step(k, carry):
-        re, im = carry
-        n = partners[t, k]
-        wr = w_ref[0, k, pl.ds(0, band, stride=2), :]
-        wi = w_ref[0, k, pl.ds(1, band, stride=2), :]
-        vr, vi = p_ref[n, 0], p_ref[n, 1]
-        return re + (vr * wr - vi * wi), im + (vr * wi + vi * wr)
-
-    zero = jnp.zeros((band, LANES), F32)
-    re, im = lax.fori_loop(0, w_ref.shape[1], step, (zero, zero), unroll=4)
-    out_ref[0, 0] = re
-    out_ref[0, 1] = im
-
-
 VM = pl.BlockSpec(memory_space=pltpu.VMEM)
 SM = pl.BlockSpec(memory_space=pltpu.SMEM)
+ANY = pl.BlockSpec(memory_space=pl.ANY)
 
 
 def body(fine_fields, fine_octant, mid_octant, shift_fine, shift_mid, interp_theta_mid, interp_phi_mid,
@@ -241,40 +367,42 @@
     at = interp_theta_top
 
     params = pltpu.CompilerParams(vmem_limit_bytes=48 * 2**20)
-    banded = pl.pallas_call(
+    subs = lax.axis_size("sub")
+    hops = subs // 4
+    dma = pltpu.SemaphoreType.DMA
+    inside = partners % tops
+    place = partners - inside + inside % slots * dirs + inside // slots
+    parent = pl.pallas_call(
         up_kernel,
         out_shape=jax.ShapeDtypeStruct((dirs, slots, 2, band, LANES), F32),
-        in_specs=[SM, SM] + [VM] * 9,
-        out_specs=VM,
+        in_specs=[SM] * 3 + [VM] * 9 + [ANY],
+        out_specs=ANY,
         scratch_shapes=[
-            pltpu.VMEM((pack, rows, LANES), F32),
-            pltpu.VMEM((mids * theta_mid, LANES), F32),
-            pltpu.VMEM((mids * theta_mid, 2 * LANES), F32),
+            pltpu.VMEM((pack, rows // slots, LANES), F32),
+            pltpu.VMEM((8 * theta_mid, LANES), F32),
+            pltpu.VMEM((8 * theta_mid, 2 * LANES), F32),
+            pltpu.VMEM((dirs, slots, 2, band, LANES), F32),
+            pltpu.VMEM((subs * tops, 2, band, LANES), F32),
+            pltpu.VMEM((tops, listed, 2 * band, LANES), F32),
+            pltpu.VMEM((tops, 2, band, LANES), F32),
+            dma((tops,)),
+            dma((slots,)),
+            dma,
+            dma((dirs, slots)),
+            dma((dirs, slots)),
+            dma((hops, slots)),
+            dma((hops, slots)),
+            dma((hops, slots)),
+            dma((hops, slots)),
+            dma((2 * hops + 1, slots)),
+            dma((2 * hops + 1, slots)),
+            dma((dirs,)),
+            dma((dirs,)),
         ],
-        compiler_params=params,
-        name="up",
-    )(fine_octant, mid_oct, x, wf, af, wt, at, cf, sf, ct, st)
-
-    received = lax.all_to_all(banded, "dir", split_axis=0, concat_axis=0, tiled=True)
-    top_fields = received.reshape(tops, 2, band, LANES)
-    portion = lax.all_gather(top_fields, "sub", axis=0, tiled=True)
-
-    top_incoming = pl.pallas_call(
-        translate_kernel,
-        out_shape=jax.ShapeDtypeStruct((tops, 2, band, LANES), F32),
-        grid=(tops,),
-        in_specs=[
-            SM,
-            VM,
-            pl.BlockSpec((1, listed, 2 * band, LANES), lambda t: (t, 0, 0, 0)),
-        ],
-        out_specs=pl.BlockSpec((1, 2, band, LANES), lambda t: (t, 0, 0, 0)),
-        compiler_params=params,
-        name="translate",
-    )(partners, portion, w)
-
-    parent = lax.all_to_all(
-        top_incoming.reshape(dirs, slots, 2, band, LANES), "dir", split_axis=0, concat_axis=0, tiled=True)
+        compiler_params=pltpu.CompilerParams(
+            vmem_limit_bytes=48 * 2**20, collective_id=0, has_side_effects=True),
+        name="rise",
+    )(fine_octant, mid_oct, place, x, wf, af, wt, at, cf, sf, ct, st, w)
 
     result = pl.pallas_call(
         down_kernel,

time: 144 us -> 75.5 us (0.52)
  waiting for transfers between devices: 50.5 us -> 0 us
  Pallas kernels: 40.8 us -> 64.5 us
  blocking collectives: 20.7 us -> 0 us
  between operations: 13.5 us -> 0.16 us
  starting transfers between devices: 4.6 us -> 0 us
  local copies, waits for them, and re-layouts: 10.4 us -> 7.64 us
    pallas_call x1, Pallas kernels: 12.5 us -> 49.8 us  [body(): pl.pallas_call(up_kernel, out_shape=jax.ShapeDtypeStruct((dirs, slots, 2,...]
    all_gather x1 -> x0, waiting for transfers between devices: 35.8 us -> none  [body(): portion = lax.all_gather(top_fields, 'sub', axis=0, tiled=True)]
    all_to_all x1 -> x0, blocking collectives: 20.7 us -> none  [body(): lax.all_to_all(banded, 'dir', split_axis=0, concat_axis=0, tiled=True)]
    all_to_all x1 -> x0, waiting for transfers between devices: 14.6 us -> none  [body(): lax.all_to_all(top_incoming.reshape(dirs, slots, 2, band, LANES), 'dir',...]
    pallas_call x1 -> x0, Pallas kernels: 13.4 us -> none  [body(): pl.pallas_call(translate_kernel, out_shape=jax.ShapeDtypeStruct((tops, 2,...]
    all_to_all x1 -> x0, starting transfers between devices: 4.6 us -> none  [body(): lax.all_to_all(top_incoming.reshape(dirs, slots, 2, band, LANES), 'dir',...]
    unnamed x17 -> x13, local copies, waits for them, and re-layouts: 6.51 us -> 3.11 us
  transfers between devices with their start and end apart: 2 -> 0, of which waited for: 2 -> 0; matrix products, arithmetic and copies ran while one was open for 0% -> 0% of each run, Pallas kernels for 0% -> 0%
where the time goes in v2:
time: 75.5 us; the launch traced here: 74.5 us
  Pallas kernels  64.5 us (85%)
  local copies, waits for them, and re-layouts  7.64 us (10%)
  other arithmetic  2.22 us (3%)
    pallas_call x1, Pallas kernels, body(): pl.pallas_call(up_kernel, out_shape=jax.ShapeDtypeStruct((dirs, slots, 2,...  49.8 us
    pallas_call x1, Pallas kernels, body(): pl.pallas_call(down_kernel, out_shape=jax.ShapeDtypeStruct((rows * 2, LAN...  14.7 us
    unnamed x13, local copies, waits for them, and re-layouts  3.11 us

profile of v2, /device:TPU:0, one launch (start us, length us, event | category | flops | bytes accessed | tf_op | source)
XLA Modules:
  0.0 74.5 jit_solution(9304942529896725500)
XLA Ops:
  0.0 0.7 dynamic_slice.3.mid_oct
  0.7 0.7 fusion.3.partners
  1.5 0.1 broadcast_multiply_fusion.2
  1.5 0.7 copy.39
  2.2 0.1 copy.25.af_ref
  2.3 0.9 %copy.26.at_ref = f32[128,64]{1,0:T(8,128)S(1)} copy(f32[128,64]{0,1:T(8,128)} %param.18) | data formatting | bytes 65536 | tf_op args[7]
  3.2 0.9 %broadcast_multiply_fusion.1 = f32[2,64,2,128]{3,2,1,0:T(2,128)S(1)} fusion(f32[64,128]{1,0:T(8,128)} %bitcast.52, f32[2,2]{1,0:T(2,128)S(1)} %compare_convert_fusion), kind=kLoop, calls=%fused_computation.8 | loop fusion | flops 32768 | bytes 163856 | tf_op jit(solution)/shard_map/mul | solution.py:366
  4.1 0.1 copy.28
  4.2 1.4 %fusion.10 = (f32[8,4096]{1,0:T(8,128)S(1)}, f32[8,4096]{1,0:T(8,128)S(1)}) fusion(f32[8,4096]{1,0:T(8,128)} %param.14), kind=kLoop, calls=%fused_computation.33 | loop fusion | bytes 393216 | tf_op jit(solution)/shard_map/sin | solution.py:355
  5.5 0.1 reshape.81
  5.7 0.0 copy-start.4
  5.7 0.1 reshape.80
  5.8 0.2 pad_maximum_fusion
  6.0 0.0 copy-start.3
  6.0 0.4 copy-done.4
  6.4 0.3 broadcast_multiply_fusion
  6.7 0.9 %mul.67.wf_ref = f32[256,512]{1,0:T(8,128)S(1)} reshape(f32[2,4,32,4,2,64]{5,4,3,2,1,0:T(2,128)S(1)} %broadcast_multiply_fusion) | data formatting | bytes 1048576 | tf_op jit(solution)/shard_map/mul | solution.py:363
  7.7 0.2 copy.27
  7.9 0.0 copy-start
  7.9 0.0 copy-start.2
  7.9 0.0 copy-done.3
  7.9 1.9 %sine_bitcast_fusion = (f32[1,8,128,128]{3,1,2,0:T(8,128)S(1)}, f32[1,8,128,128]{3,1,2,0:T(8,128)S(1)}) fusion(f32[8,16384]{1,0:T(8,128)S(1)} %copy-done.3), kind=kLoop, calls=%fused_computation.2 | loop fusion | bytes 1572864
  9.8 0.2 copy_bitcast_fusion
  10.0 0.0 copy-done
  10.0 0.0 copy-done.2
  10.0 0.0 copy-start.1
  10.0 49.8 %rise.1.r_ref = f32[4,4,2,32,128]{4,3,2,1,0:T(8,128)S(1)} custom-call(s32[256]{0:T(256)S(1)} %copy-done.2, s32[32]{0:T(128)S(1)} %dynamic_slice.3.mid_oct, s32[16,32]{1,0:T(8,128)S(1)} %fusion.3.partners, f32[4096,128]{1,0:T(8,128)S(1)} %bitcast.42, f32[256,512]{1,0:T(8,128)S(1)} %mul.67.wf_ref, f32[64,32]{1,0:T(8,128)S(1)} %copy.25.af_ref, ...), custom_call_target="tpu_custom_call" | custom-call | tf_op jit(solution)/shard_map/rise/pallas_call | solution.py:375
  59.8 0.0 copy-done.1
  59.9 14.7 %down.1 = f32[4096,128]{1,0:T(8,128)} custom-call(s32[256]{0:T(256)S(1)} %copy-done.2, s32[32]{0:T(128)S(1)} %dynamic_slice.3.mid_oct, f32[4,4,2,32,128]{4,3,2,1,0:T(8,128)S(1)} %rise.1.r_ref, f32[512,256]{1,0:T(8,128)S(1)} %bitcast.43, f32[32,64]{1,0:T(8,128)S(1)} %bitcast.48, f32[256,128]{1,0:T(8,128)S(1)} %bitcast.46, f32[64,128]{1,0:T(8,128)S(1)} %bitcast.49, ...), custom_call_target="tpu_custom_call" | custom-call | tf_op jit(solution)/shard_map/down/pallas_call | solution.py:407
  (4 shorter events, 0.0 us)
Async XLA Ops:
  5.7 0.7 copy-start.4
  6.0 1.9 %copy-start.3 = (f32[8,16384]{1,0:T(8,128)S(1)}, f32[8,16384]{1,0:T(8,128)}, u32[]{:S(2)}) copy-start(f32[8,16384]{1,0:T(8,128)} %param.15) | copy-start | bytes 1572868
  7.9 2.1 %copy-start = (f32[256,2,1024]{2,1,0:T(2,128)S(1)}, f32[256,2,1024]{2,1,0:T(2,128)}, u32[]{:S(2)}) copy-start(f32[256,2,1024]{2,1,0:T(2,128)} %param.11) | copy-start | bytes 6291460
  7.9 2.1 %copy-start.2 = (s32[256]{0:T(256)S(1)}, s32[256]{0:T(256)}, u32[]{:S(2)}) copy-start(s32[256]{0:T(256)} %fine_oct.3) | copy-start | bytes 3076
  10.0 49.9 %copy-start.1 = (f32[128,64]{0,1:T(8,128)S(1)}, f32[128,64]{0,1:T(8,128)}, u32[]{:S(2)}) copy-start(f32[128,64]{0,1:T(8,128)} %param.18) | copy-start | bytes 98308

commit v3 on v2

--- a/solution.py
+++ b/solution.py
@@ -35,6 +35,24 @@
     return jnp.concatenate([hi, hi, lo], axis=0)
 
 
+def wide_dot_t(x, w_hi, w_lo):
+    def mt(a, b):
+        return lax.dot_general(a, b, (((1,), (1,)), ((), ())), preferred_element_type=F32)
+
+    hi, lo = split(x)
+    return mt(hi, w_hi) + (mt(hi, w_lo) + mt(lo, w_hi))
+
+
+def twice(b):
+    zero = jnp.zeros_like(b)
+    return jnp.concatenate([jnp.concatenate([b, zero], axis=1), jnp.concatenate([zero, b], axis=1)], axis=0)
+
+
+def banded_rows(af_ref, pack):
+    per = af_ref.shape[0] // pack
+    return jnp.concatenate([af_ref[pl.ds(a, per, stride=pack), :] for a in range(pack)], axis=0)
+
+
 def chunk_of(rows):
     return min(rows, 512)
 
@@ -45,7 +63,7 @@
               part_send, part_recv, r_send, r_recv):
     pack, step, _ = y_ref.shape
     theta_mid = cf_ref.shape[1]
-    theta_fine = af_ref.shape[1]
+    theta_fine = af_ref.shape[0]
     per = theta_fine // pack
     half = LANES // 2
     dirs, slots, _, band, _ = banded_ref.shape
@@ -120,9 +138,9 @@
             copy.start()
 
     wf_hi, wf_lo = split(wf_ref[...])
-    wt_hi, wt_lo = split(wt_ref[...])
-    a_mid = left3(af_ref[...])
-    a_top = left3(at_ref[...])
+    wt_hi, wt_lo = split(twice(wt_ref[...]))
+    a_mid = left3(banded_rows(af_ref, pack).T)
+    a_top = left3(at_ref[...].T)
     banded_ref[...] = jnp.zeros_like(banded_ref)
 
     @pl.loop(0, slots)
@@ -164,7 +182,7 @@
         z_ref[...] = wide_dot(mid_ref[...], wt_hi, wt_lo)
 
         def top_step(m, carry):
-            o = mid_oct[q * 8 + m]
+            o = mid_oct[(z * slots + q) * 8 + m]
             v = mm(a_top, right3(z_ref[pl.ds(pl.multiple_of(m * theta_mid, theta_mid), theta_mid), :]))
             for d in range(dirs):
                 at = slice(d * band, (d + 1) * band)
@@ -217,6 +235,8 @@
         def one(k, carry):
             re, im = carry
             n = partners[t, k]
+            inside = lax.rem(n, tops)
+            n = n - inside + lax.rem(inside, slots) * dirs + lax.div(inside, slots)
             wr = w_ref[t, k, pl.ds(0, band, stride=2), :]
             wi = w_ref[t, k, pl.ds(1, band, stride=2), :]
             vr, vi = p_ref[n, 0], p_ref[n, 1]
@@ -265,6 +285,7 @@
     per = theta_fine // pack
     mids = mid_ref.shape[0] // theta_mid
     dirs = r_ref.shape[0]
+    first_mid = lax.axis_index("dir") * mids
     half = LANES // 2
 
     a_hi, a_lo = split(at_ref[...])
@@ -273,7 +294,7 @@
 
     def top_step(m, carry):
         q = m // 8
-        o = mid_oct[m]
+        o = mid_oct[first_mid + m]
         c, s = ct_ref[o], st_ref[o]
         re = jnp.concatenate([r_ref[d, q, 0] for d in range(dirs)], axis=0)
         im = jnp.concatenate([r_ref[d, q, 1] for d in range(dirs)], axis=0)
@@ -284,16 +305,16 @@
 
     lax.fori_loop(0, mids, top_step, 0, unroll=2)
 
-    wt_hi, wt_lo = split(wt_ref[...])
+    wt_hi, wt_lo = split(twice(wt_ref[...]))
     mid_rows = mids * theta_mid
     step2 = chunk_of(mid_rows)
 
     @pl.loop(0, mid_rows // step2)
     def _(i):
         base = pl.multiple_of(i * step2, 8)
-        mid_ref[pl.ds(base, step2), :] = wide_dot(z_ref[pl.ds(base, step2), :], wt_hi, wt_lo)
-
-    a_mid = left3(af_ref[...])
+        mid_ref[pl.ds(base, step2), :] = wide_dot_t(z_ref[pl.ds(base, step2), :], wt_hi, wt_lo)
+
+    a_mid = left3(banded_rows(af_ref, pack))
 
     def mid_step(m, carry):
         v = mid_ref[pl.ds(pl.multiple_of(m * theta_mid, theta_mid), theta_mid), :]
@@ -346,7 +367,6 @@
     per = theta_fine // pack
     rows = boxes * per
 
-    mid_oct = lax.dynamic_slice_in_dim(mid_octant, lax.axis_index("dir") * mids, mids)
     x = fine_fields.reshape(boxes, 2, per, LANES).transpose(0, 2, 1, 3).reshape(rows * 2, LANES)
     w = translation.reshape(tops, listed, 2, band, LANES).transpose(0, 1, 3, 2, 4).reshape(
         tops, listed, 2 * band, LANES)
@@ -362,16 +382,12 @@
     lots = jnp.eye(pack, dtype=F32)
     wf = (two[:, None, None, None, :, None] * lots[None, :, None, :, None, None]
           * interp_phi_mid.T[None, None, :, None, None, :]).reshape(2 * LANES, pack * 2 * phi_mid)
-    af = interp_theta_mid.reshape(theta_mid, per, pack).transpose(0, 2, 1).reshape(theta_mid, theta_fine)
-    wt = (two[:, None, :, None] * interp_phi_top.T[None, :, None, :]).reshape(2 * phi_mid, 2 * phi_top)
-    at = interp_theta_top
+    af, wt, at = interp_theta_mid.T, interp_phi_top.T, interp_theta_top.T
 
     params = pltpu.CompilerParams(vmem_limit_bytes=48 * 2**20)
     subs = lax.axis_size("sub")
     hops = subs // 4
     dma = pltpu.SemaphoreType.DMA
-    inside = partners % tops
-    place = partners - inside + inside % slots * dirs + inside // slots
     parent = pl.pallas_call(
         up_kernel,
         out_shape=jax.ShapeDtypeStruct((dirs, slots, 2, band, LANES), F32),
@@ -402,7 +418,7 @@
         compiler_params=pltpu.CompilerParams(
             vmem_limit_bytes=48 * 2**20, collective_id=0, has_side_effects=True),
         name="rise",
-    )(fine_octant, mid_oct, place, x, wf, af, wt, at, cf, sf, ct, st, w)
+    )(fine_octant, mid_octant, partners, x, wf, af, wt, at, cf, sf, ct, st, w)
 
     result = pl.pallas_call(
         down_kernel,
@@ -416,7 +432,7 @@
         ],
         compiler_params=params,
         name="down",
-    )(fine_octant, mid_oct, parent, wf.T, af.T, wt.T, at.T, cf, sf, ct, st)
+    )(fine_octant, mid_octant, parent, wf.T, af, wt, at, cf, sf, ct, st)
     return result.reshape(boxes, per, 2, LANES).transpose(0, 2, 1, 3).reshape(boxes, 2, theta_fine * phi_fine)
 
 

time: 75.5 us -> 71.5 us (0.947)
  local copies, waits for them, and re-layouts: 7.64 us -> 4.82 us
  other arithmetic: 2.22 us -> 0.64 us
    unnamed x13 -> x19, local copies, waits for them, and re-layouts: 3.11 us -> 1.91 us
    mul x1 -> x0, other arithmetic: 0.87 us -> none  [body(): two[:, None, :, None] * interp_phi_top.T[None, :, None, :]]
    reshape x2 -> x0, local copies, waits for them, and re-layouts: 0.8 us -> none  [body(): interp_theta_mid.reshape(theta_mid, per, pack).transpose(0, 2, 1)]
where the time goes in v3:
time: 71.5 us; the launch traced here: 70.7 us
  Pallas kernels  65.1 us (91%)
  local copies, waits for them, and re-layouts  4.82 us (7%)
    pallas_call x1, Pallas kernels, body(): pl.pallas_call(up_kernel, out_shape=jax.ShapeDtypeStruct((dirs, slots, 2,...  50.4 us
    pallas_call x1, Pallas kernels, body(): pl.pallas_call(down_kernel, out_shape=jax.ShapeDtypeStruct((rows * 2, LAN...  14.7 us
    unnamed x19, local copies, waits for them, and re-layouts  1.91 us

profile of v3, /device:TPU:0, one launch (start us, length us, event | category | flops | bytes accessed | tf_op | source)
XLA Modules:
  0.0 70.7 jit_solution(2034481301223340733)
XLA Ops:
  0.0 0.0 copy-start.8
  0.0 0.1 broadcast_multiply_fusion.1
  0.1 1.4 %fusion.1 = (f32[8,4096]{1,0:T(8,128)S(1)}, f32[8,4096]{1,0:T(8,128)S(1)}) fusion(f32[8,4096]{1,0:T(8,128)} %param.14), kind=kLoop, calls=%fused_computation.11 | loop fusion | bytes 393216 | tf_op jit(solution)/shard_map/sin | solution.py:375
  1.5 0.1 reshape.60
  1.6 0.1 reshape.59
  1.7 0.2 pad_maximum_fusion
  1.9 0.0 copy-start.7
  1.9 0.0 copy-done.8
  1.9 0.3 broadcast_multiply_fusion
  2.3 0.9 %mul.41.wf_ref = f32[256,512]{1,0:T(8,128)S(1)} reshape(f32[2,4,32,4,2,64]{5,4,3,2,1,0:T(2,128)S(1)} %broadcast_multiply_fusion) | data formatting | bytes 1048576 | tf_op jit(solution)/shard_map/mul | solution.py:383
  3.2 0.2 copy.19
  3.4 0.0 copy-start
  3.4 0.0 copy-start.1
  3.4 0.0 copy-start.2
  3.4 0.0 copy-start.3
  3.5 0.0 copy-start.4
  3.5 0.0 copy-start.5
  3.5 0.0 copy-start.6
  3.5 0.0 copy-done.7
  3.5 1.9 %sine_bitcast_fusion = (f32[1,8,128,128]{3,1,2,0:T(8,128)S(1)}, f32[1,8,128,128]{3,1,2,0:T(8,128)S(1)}) fusion(f32[8,16384]{1,0:T(8,128)S(1)} %copy-done.7), kind=kLoop, calls=%fused_computation.2 | loop fusion | bytes 1572864
  5.4 0.2 copy_bitcast_fusion
  5.6 0.0 copy-done
  5.6 0.0 copy-done.1
  5.6 0.0 copy-done.2
  5.6 0.0 copy-done.3
  5.6 0.0 copy-done.4
  5.6 0.0 copy-done.5
  5.6 0.0 copy-done.6
  5.7 50.4 %rise.1.r_ref = f32[4,4,2,32,128]{4,3,2,1,0:T(8,128)S(1)} custom-call(s32[256]{0:T(256)S(1)} %copy-done.5, s32[128]{0:T(128)S(1)} %copy-done.6, s32[16,32]{1,0:T(8,128)S(1)} %copy-done.4, f32[4096,128]{1,0:T(8,128)S(1)} %bitcast.28, f32[256,512]{1,0:T(8,128)S(1)} %mul.41.wf_ref, f32[32,64]{1,0:T(8,128)S(1)} %bitcast.34, f32[64,128]{1,0:T(8,128)S(1)} %bitcast.30, ...), custom_call_target="tpu_custom_call" | custom-call | tf_op jit(solution)/shard_map/rise/pallas_call | solution.py:391
  56.1 14.7 %down.1 = f32[4096,128]{1,0:T(8,128)} custom-call(s32[256]{0:T(256)S(1)} %copy-done.5, s32[128]{0:T(128)S(1)} %copy-done.6, f32[4,4,2,32,128]{4,3,2,1,0:T(8,128)S(1)} %rise.1.r_ref, f32[512,256]{1,0:T(8,128)S(1)} %bitcast.29, f32[32,64]{1,0:T(8,128)S(1)} %bitcast.35, f32[64,128]{1,0:T(8,128)S(1)} %bitcast.31, f32[64,128]{1,0:T(8,128)S(1)} %bitcast.33, ...), custom_call_target="tpu_custom_call" | custom-call | tf_op jit(solution)/shard_map/down/pallas_call | solution.py:423
  (3 shorter events, 0.0 us)
Async XLA Ops:
  0.0 1.9 %copy-start.8 = (f32[64,32]{0,1:T(8,128)S(1)}, f32[64,32]{0,1:T(8,128)}, u32[]{:S(2)}) copy-start(f32[64,32]{0,1:T(8,128)} %param.17) | copy-start | bytes 24580
  1.9 1.6 %copy-start.7 = (f32[8,16384]{1,0:T(8,128)S(1)}, f32[8,16384]{1,0:T(8,128)}, u32[]{:S(2)}) copy-start(f32[8,16384]{1,0:T(8,128)} %param.15) | copy-start | bytes 1572868
  3.4 2.2 %copy-start = (f32[256,2,1024]{2,1,0:T(2,128)S(1)}, f32[256,2,1024]{2,1,0:T(2,128)}, u32[]{:S(2)}) copy-start(f32[256,2,1024]{2,1,0:T(2,128)} %param.11) | copy-start | bytes 6291460
  3.4 2.2 %copy-start.1 = (f32[128,64]{0,1:T(8,128)S(1)}, f32[128,64]{0,1:T(8,128)}, u32[]{:S(2)}) copy-start(f32[128,64]{0,1:T(8,128)} %param.19) | copy-start | bytes 98308
  3.4 2.2 %copy-start.2 = (f32[128,64]{0,1:T(8,128)S(1)}, f32[128,64]{0,1:T(8,128)}, u32[]{:S(2)}) copy-start(f32[128,64]{0,1:T(8,128)} %param.18) | copy-start | bytes 98308
  3.4 2.2 %copy-start.3 = (f32[64,32]{0,1:T(8,128)S(1)}, f32[64,32]{0,1:T(8,128)}, u32[]{:S(2)}) copy-start(f32[64,32]{0,1:T(8,128)} %param.16) | copy-start | bytes 24580
  3.5 2.2 %copy-start.4 = (s32[16,32]{1,0:T(8,128)S(1)}, s32[16,32]{1,0:T(8,128)}, u32[]{:S(2)}) copy-start(s32[16,32]{1,0:T(8,128)} %partners.1) | copy-start | bytes 6148
  3.5 2.2 %copy-start.5 = (s32[256]{0:T(256)S(1)}, s32[256]{0:T(256)}, u32[]{:S(2)}) copy-start(s32[256]{0:T(256)} %fine_oct.3) | copy-start | bytes 3076
  3.5 2.2 %copy-start.6 = (s32[128]{0:T(128)S(1)}, s32[128]{0:T(128)}, u32[]{:S(2)}) copy-start(s32[128]{0:T(128)} %mid_oct.3) | copy-start | bytes 1540

commit v4 on v3

--- a/solution.py
+++ b/solution.py
@@ -178,7 +178,7 @@
             mid_ref[pl.ds(pl.multiple_of(m * theta_mid, theta_mid), theta_mid), :] = acc1 + pltpu.roll(acc2, half, 1)
             return carry
 
-        lax.fori_loop(0, 8, mid_step, 0, unroll=2)
+        lax.fori_loop(0, 8, mid_step, 0, unroll=4)
         z_ref[...] = wide_dot(mid_ref[...], wt_hi, wt_lo)
 
         def top_step(m, carry):
@@ -192,7 +192,7 @@
                 banded_ref[d, q, 1] += re * s + im * c
             return carry
 
-        lax.fori_loop(0, 8, top_step, 0, unroll=2)
+        lax.fori_loop(0, 8, top_step, 0, unroll=4)
 
     if slots > 1:
         own_ship(slots - 2)
@@ -303,7 +303,7 @@
         z_ref[pl.ds(pl.multiple_of(m * theta_mid, theta_mid), theta_mid), :] = z[:theta_mid] + z[theta_mid:]
         return carry
 
-    lax.fori_loop(0, mids, top_step, 0, unroll=2)
+    lax.fori_loop(0, mids, top_step, 0, unroll=4)
 
     wt_hi, wt_lo = split(twice(wt_ref[...]))
     mid_rows = mids * theta_mid
@@ -332,7 +332,7 @@
                     y_ref[a, pl.ds(start, per), :] = z[a * per:(a + 1) * per, side * LANES:(side + 1) * LANES]
         return carry
 
-    lax.fori_loop(0, mids, mid_step, 0, unroll=2)
+    lax.fori_loop(0, mids, mid_step, 0, unroll=4)
 
     wf_hi, wf_lo = split(wf_ref[...])
     step = chunk_of(rows)

time: 71.5 us -> 68.2 us (0.954)
  Pallas kernels: 65.1 us -> 61.7 us
    pallas_call x1, Pallas kernels: 14.7 us -> 12.1 us  [body(): pl.pallas_call(down_kernel, out_shape=jax.ShapeDtypeStruct((rows * 2, LAN...]
    pallas_call x1, Pallas kernels: 50.4 us -> 49.6 us  [body(): pl.pallas_call(up_kernel, out_shape=jax.ShapeDtypeStruct((dirs, slots, 2,...]
where the time goes in v4:
time: 68.2 us; the launch traced here: 67.4 us
  Pallas kernels  61.7 us (90%)
  local copies, waits for them, and re-layouts  4.82 us (7%)
    pallas_call x1, Pallas kernels, body(): pl.pallas_call(up_kernel, out_shape=jax.ShapeDtypeStruct((dirs, slots, 2,...  49.6 us
    pallas_call x1, Pallas kernels, body(): pl.pallas_call(down_kernel, out_shape=jax.ShapeDtypeStruct((rows * 2, LAN...  12.1 us
    unnamed x19, local copies, waits for them, and re-layouts  1.91 us
    sin x1, local copies, waits for them, and re-layouts, body(): sin_f = jnp.sin(shift_fine).reshape(8, theta_mid, phi_mid)  1.37 us

profile of v4, /device:TPU:0, one launch (start us, length us, event | category | flops | bytes accessed | tf_op | source)
XLA Modules:
  0.0 67.4 jit_solution(9682383954743132011)
XLA Ops:
  0.0 0.0 copy-start.8
  0.0 0.1 broadcast_multiply_fusion.1
  0.1 1.4 %fusion.1 = (f32[8,4096]{1,0:T(8,128)S(1)}, f32[8,4096]{1,0:T(8,128)S(1)}) fusion(f32[8,4096]{1,0:T(8,128)} %param.14), kind=kLoop, calls=%fused_computation.11 | loop fusion | bytes 393216 | tf_op jit(solution)/shard_map/sin | solution.py:375
  1.5 0.1 reshape.60
  1.6 0.1 reshape.59
  1.7 0.2 pad_maximum_fusion
  1.9 0.0 copy-start.7
  1.9 0.0 copy-done.8
  1.9 0.3 broadcast_multiply_fusion
  2.3 0.9 %mul.41.wf_ref = f32[256,512]{1,0:T(8,128)S(1)} reshape(f32[2,4,32,4,2,64]{5,4,3,2,1,0:T(2,128)S(1)} %broadcast_multiply_fusion) | data formatting | bytes 1048576 | tf_op jit(solution)/shard_map/mul | solution.py:383
  3.2 0.2 copy.19
  3.4 0.0 copy-start
  3.4 0.0 copy-start.1
  3.4 0.0 copy-start.2
  3.4 0.0 copy-start.3
  3.5 0.0 copy-start.4
  3.5 0.0 copy-start.5
  3.5 0.0 copy-start.6
  3.5 0.0 copy-done.7
  3.5 1.9 %sine_bitcast_fusion = (f32[1,8,128,128]{3,1,2,0:T(8,128)S(1)}, f32[1,8,128,128]{3,1,2,0:T(8,128)S(1)}) fusion(f32[8,16384]{1,0:T(8,128)S(1)} %copy-done.7), kind=kLoop, calls=%fused_computation.2 | loop fusion | bytes 1572864
  5.4 0.2 copy_bitcast_fusion
  5.6 0.0 copy-done
  5.6 0.0 copy-done.1
  5.6 0.0 copy-done.2
  5.6 0.0 copy-done.3
  5.6 0.0 copy-done.4
  5.6 0.0 copy-done.5
  5.6 0.0 copy-done.6
  5.7 49.6 %rise.1.r_ref = f32[4,4,2,32,128]{4,3,2,1,0:T(8,128)S(1)} custom-call(s32[256]{0:T(256)S(1)} %copy-done.5, s32[128]{0:T(128)S(1)} %copy-done.6, s32[16,32]{1,0:T(8,128)S(1)} %copy-done.4, f32[4096,128]{1,0:T(8,128)S(1)} %bitcast.28, f32[256,512]{1,0:T(8,128)S(1)} %mul.41.wf_ref, f32[32,64]{1,0:T(8,128)S(1)} %bitcast.34, f32[64,128]{1,0:T(8,128)S(1)} %bitcast.30, ...), custom_call_target="tpu_custom_call" | custom-call | tf_op jit(solution)/shard_map/rise/pallas_call | solution.py:391
  55.3 12.1 %down.1 = f32[4096,128]{1,0:T(8,128)} custom-call(s32[256]{0:T(256)S(1)} %copy-done.5, s32[128]{0:T(128)S(1)} %copy-done.6, f32[4,4,2,32,128]{4,3,2,1,0:T(8,128)S(1)} %rise.1.r_ref, f32[512,256]{1,0:T(8,128)S(1)} %bitcast.29, f32[32,64]{1,0:T(8,128)S(1)} %bitcast.35, f32[64,128]{1,0:T(8,128)S(1)} %bitcast.31, f32[64,128]{1,0:T(8,128)S(1)} %bitcast.33, ...), custom_call_target="tpu_custom_call" | custom-call | tf_op jit(solution)/shard_map/down/pallas_call | solution.py:423
  (3 shorter events, 0.0 us)
Async XLA Ops:
  0.0 1.9 %copy-start.8 = (f32[64,32]{0,1:T(8,128)S(1)}, f32[64,32]{0,1:T(8,128)}, u32[]{:S(2)}) copy-start(f32[64,32]{0,1:T(8,128)} %param.17) | copy-start | bytes 24580
  1.9 1.6 %copy-start.7 = (f32[8,16384]{1,0:T(8,128)S(1)}, f32[8,16384]{1,0:T(8,128)}, u32[]{:S(2)}) copy-start(f32[8,16384]{1,0:T(8,128)} %param.15) | copy-start | bytes 1572868
  3.4 2.2 %copy-start = (f32[256,2,1024]{2,1,0:T(2,128)S(1)}, f32[256,2,1024]{2,1,0:T(2,128)}, u32[]{:S(2)}) copy-start(f32[256,2,1024]{2,1,0:T(2,128)} %param.11) | copy-start | bytes 6291460
  3.4 2.2 %copy-start.1 = (f32[128,64]{0,1:T(8,128)S(1)}, f32[128,64]{0,1:T(8,128)}, u32[]{:S(2)}) copy-start(f32[128,64]{0,1:T(8,128)} %param.19) | copy-start | bytes 98308
  3.4 2.2 %copy-start.2 = (f32[128,64]{0,1:T(8,128)S(1)}, f32[128,64]{0,1:T(8,128)}, u32[]{:S(2)}) copy-start(f32[128,64]{0,1:T(8,128)} %param.18) | copy-start | bytes 98308
  3.4 2.2 %copy-start.3 = (f32[64,32]{0,1:T(8,128)S(1)}, f32[64,32]{0,1:T(8,128)}, u32[]{:S(2)}) copy-start(f32[64,32]{0,1:T(8,128)} %param.16) | copy-start | bytes 24580
  3.5 2.2 %copy-start.4 = (s32[16,32]{1,0:T(8,128)S(1)}, s32[16,32]{1,0:T(8,128)}, u32[]{:S(2)}) copy-start(s32[16,32]{1,0:T(8,128)} %partners.1) | copy-start | bytes 6148
  3.5 2.2 %copy-start.5 = (s32[256]{0:T(256)S(1)}, s32[256]{0:T(256)}, u32[]{:S(2)}) copy-start(s32[256]{0:T(256)} %fine_oct.3) | copy-start | bytes 3076
  3.5 2.2 %copy-start.6 = (s32[128]{0:T(128)S(1)}, s32[128]{0:T(128)}, u32[]{:S(2)}) copy-start(s32[128]{0:T(128)} %mid_oct.3) | copy-start | bytes 1540
